TPU v7x, 256 devices: a whole 4x4x8 slice. The times are simulated.
256 devices in a mesh: guide: 2 (over core), batch: 4 (over x), tensor: 32 (over z, y).
Axes of the slice: x: 4, y: 4, z: 8, core: 2. Of those that a mesh axis runs over, the one named last changes fastest.
Arguments:
- hidden_new: bfloat16 [2, 512, 2048], P('guide', ('batch', 'tensor')), may hold values from -6 to 6
- stored_rows: bfloat16 [2, 512, 24, 2048], P('guide', ('batch', 'tensor')), may hold values from -6 to 6
- key_cache: bfloat16 [2, 512, 288, 512], P('guide', ('batch', 'tensor')), as said below
- value_cache: bfloat16 [2, 512, 288, 512], P('guide', ('batch', 'tensor')), may hold values from -6 to 6
- lengths: int32 [2, 512], P('guide', ('batch', 'tensor')), may hold values from 72 to 287, as said below
- recompute_blocks: int32 [2, 512, 2], P('guide', ('batch', 'tensor')), may hold values from 0 to 22, as said below
- prefill_flags: int32 [512], P(('batch', 'tensor')), may hold values 0 or 1
- guidance: int32 [2], replicated, may hold values from 2 to 15
- attn_gain: float32 [2048], replicated, may hold values from 0.5 to 1.5
- query_gain: float32 [64], replicated, may hold values from 0.5 to 2
- key_gain: float32 [64], replicated, may hold values from 0.5 to 1.5
- final_gain: float32 [2048], replicated, may hold values from 0.5 to 1.5
- w_query: bfloat16 [2048, 2048], P(None, 'tensor'), may hold values from -0.125 to 0.125
- w_key: bfloat16 [2048, 512], P(None, 'tensor'), may hold values from -0.125 to 0.125
- w_value: bfloat16 [2048, 512], P(None, 'tensor'), may hold values from -0.125 to 0.125
- w_out: bfloat16 [2048, 2048], P('tensor'), may hold values from -0.125 to 0.125
- w_vocab: bfloat16 [2048, 65536], P(None, ('guide', 'batch', 'tensor')), may hold values from -0.125 to 0.125
Outputs:
- hidden_out: bfloat16 [2, 512, 2048], P('guide', ('batch', 'tensor'))
- key_out: bfloat16 [2, 512, 288, 512], P('guide', ('batch', 'tensor'))
- value_out: bfloat16 [2, 512, 288, 512], P('guide', ('batch', 'tensor'))
- guided: float32 [512, 65536], P(None, ('guide', 'batch', 'tensor'))
Inputs may be any that keep to these rules, and one draw needn't show every extreme that they name: Each request's new token is written to cache row lengths, so lengths stay below 288; some request has 287 cached rows. `recompute_blocks`: the 2 block numbers of a request are different and each block lies wholly below that request's length. `key_cache`: finite values.
All inputs are finite; a program needn't handle non-finite values. No bound on the sum of `prefill_flags` on one device may be relied on, other than what follows from the above.
Results may differ from a plain program's by a relative error of at most 0.02.
Values may be sent and summed in bfloat16 or wider, within the bound.
No kernel may reach another device: no remote copies, remote signals or barrier semaphores. Data moves between devices by JAX's collectives and lax.ppermute only.
A program may use at most 128 MiB of HBM per device.

v0:
```python
import jax
import jax.numpy as jnp
from jax import lax
from jax.sharding import PartitionSpec as P


def rms_rows(values, gain_row):
    widened = values.astype(jnp.float32)
    return (
        widened * lax.rsqrt(jnp.mean(widened * widened, axis=-1, keepdims=True) + 1e-05) * gain_row
    )


def head_rms(values, gain_row, head_width):
    old_shape = values.shape
    split_heads = values.reshape(old_shape[:-1] + (old_shape[-1] // head_width, head_width))
    normed = (
        split_heads
        * lax.rsqrt(jnp.mean(split_heads * split_heads, axis=-1, keepdims=True) + 1e-05)
        * gain_row
    )
    return normed.reshape(old_shape)


def write_rows(cache_one, pos_one, rows_one, len_one, row_new):
    return cache_one.at[pos_one].set(rows_one).at[len_one].set(row_new)


def local(
    hidden_new,
    stored_rows,
    key_cache,
    value_cache,
    lengths,
    recompute_blocks,
    prefill_flags,
    guidance,
    attn_gain,
    query_gain,
    key_gain,
    final_gain,
    w_query,
    w_key,
    w_value,
    w_out,
    w_vocab,
):
    local_rows = hidden_new.shape[1]
    model_width = hidden_new.shape[2]
    recompute = stored_rows.shape[2]
    cache_len = key_cache.shape[2]
    kv_width = key_cache.shape[3]
    head_size = query_gain.shape[0]
    tensor_count = lax.axis_size("tensor")
    x_rows = hidden_new[0]
    normed_new = rms_rows(x_rows, attn_gain).astype(jnp.bfloat16)
    normed_old = (
        rms_rows(stored_rows[0], attn_gain)
        .astype(jnp.bfloat16)
        .reshape(local_rows * recompute, model_width)
    )
    kv_rows = jnp.concatenate([normed_old, normed_new], axis=0)
    gathered = lax.all_gather(kv_rows, "tensor", axis=0, tiled=True)
    per_device = gathered.reshape(tensor_count, local_rows * (recompute + 1), model_width)
    fresh_rows = per_device[:, local_rows * recompute :, :].reshape(
        tensor_count * local_rows, model_width
    )
    query_part = head_rms(
        jnp.dot(fresh_rows, w_query, preferred_element_type=jnp.float32), query_gain, head_size
    ).astype(jnp.bfloat16)
    kv_cols = jnp.concatenate([w_key, w_value], axis=1)
    kv_part = jnp.dot(gathered, kv_cols, preferred_element_type=jnp.float32).astype(jnp.bfloat16)
    query_all, kv_back = (
        lax.all_to_all(query_part, "tensor", split_axis=0, concat_axis=1, tiled=True),
        lax.all_to_all(kv_part, "tensor", split_axis=0, concat_axis=1, tiled=True),
    )
    slice_width = w_key.shape[1]
    kv_back = kv_back.reshape(kv_back.shape[0], tensor_count, 2, slice_width)
    keys_raw = kv_back[:, :, 0, :].reshape(-1, kv_width)
    values_all = kv_back[:, :, 1, :].reshape(-1, kv_width)
    keys_all = head_rms(keys_raw.astype(jnp.float32), key_gain, head_size).astype(jnp.bfloat16)
    split_at = local_rows * recompute
    keys_old = keys_all[:split_at].reshape(local_rows, recompute, kv_width)
    keys_new = keys_all[split_at:]
    values_old = values_all[:split_at].reshape(local_rows, recompute, kv_width)
    values_new = values_all[split_at:]
    block_count = recompute_blocks.shape[2]
    block_len = recompute // block_count
    positions = (
        jnp.repeat(recompute_blocks[0], block_len, axis=1) * block_len
        + jnp.tile(jnp.arange(block_len, dtype=jnp.int32), block_count)[None, :]
    )
    own_lengths = lengths[0]
    new_keys = jax.vmap(write_rows)(key_cache[0], positions, keys_old, own_lengths, keys_new)
    new_values = jax.vmap(write_rows)(
        value_cache[0], positions, values_old, own_lengths, values_new
    )
    kv_heads = kv_width // head_size
    head_count = query_all.shape[1] // head_size
    group_size = head_count // kv_heads
    query_heads = query_all.reshape(local_rows, kv_heads, group_size, head_size)
    key_heads = new_keys.reshape(local_rows, cache_len, kv_heads, head_size)
    value_heads = new_values.reshape(local_rows, cache_len, kv_heads, head_size)
    scores = jnp.einsum(
        "rkgd,rjkd->rkgj", query_heads, key_heads, preferred_element_type=jnp.float32
    ) * head_size ** (-0.5)
    columns = jnp.arange(cache_len, dtype=jnp.int32)
    length_col = own_lengths[:, None, None, None]
    flag_col = prefill_flags[:, None, None, None]
    visible = (columns < length_col) & (flag_col == 0) | (columns == length_col)
    scores = jnp.where(visible, scores, -1e30)
    row_max = jnp.max(scores, axis=-1, keepdims=True)
    powers = jnp.exp(scores - row_max)
    attn_probs = (powers / jnp.sum(powers, axis=-1, keepdims=True)).astype(jnp.bfloat16)
    attended = jnp.einsum(
        "rkgj,rjkd->rkgd", attn_probs, value_heads, preferred_element_type=jnp.float32
    ).astype(jnp.bfloat16)
    attended = attended.reshape(local_rows, head_count * head_size)
    by_head = lax.all_to_all(attended, "tensor", split_axis=1, concat_axis=0, tiled=True)
    projected = lax.psum_scatter(
        jnp.dot(by_head, w_out, preferred_element_type=jnp.float32).astype(jnp.bfloat16),
        "tensor",
        scatter_dimension=0,
        tiled=True,
    ).astype(jnp.float32)
    residual = (x_rows.astype(jnp.float32) + projected).astype(jnp.bfloat16)
    normed_final = rms_rows(residual, final_gain).astype(jnp.bfloat16)
    weight = guidance[0].astype(jnp.float32) / guidance[1].astype(jnp.float32)
    logits = jnp.dot(
        lax.all_gather(normed_final, ("guide", "batch", "tensor"), axis=0, tiled=True),
        w_vocab,
        preferred_element_type=jnp.float32,
    ).astype(jnp.bfloat16)
    half_rows = logits.shape[0] // 2
    cond_logits = logits[:half_rows].astype(jnp.float32)
    uncond_logits = logits[half_rows:].astype(jnp.float32)
    guided = uncond_logits + weight * (cond_logits - uncond_logits)
    return (residual[None], new_keys[None], new_values[None], guided)


def solution(mesh):
    in_specs = (
        P("guide", ("batch", "tensor"), None),
        P("guide", ("batch", "tensor"), None, None),
        P("guide", ("batch", "tensor"), None, None),
        P("guide", ("batch", "tensor"), None, None),
        P("guide", ("batch", "tensor")),
        P("guide", ("batch", "tensor"), None),
        P(("batch", "tensor")),
        P(),
        P(),
        P(),
        P(),
        P(),
        P(None, "tensor"),
        P(None, "tensor"),
        P(None, "tensor"),
        P("tensor", None),
        P(None, ("guide", "batch", "tensor")),
    )
    out_specs = (
        P("guide", ("batch", "tensor"), None),
        P("guide", ("batch", "tensor"), None, None),
        P("guide", ("batch", "tensor"), None, None),
        P(None, ("guide", "batch", "tensor")),
    )
    return jax.shard_map(local, mesh=mesh, in_specs=in_specs, out_specs=out_specs, check_vma=False)
```

profile of v0, /device:TPU:1, one launch (start us, length us, event | category | flops | bytes accessed | tf_op | source)
XLA Modules:
  0.0 512.9 jit_solution(961887310020862374)
XLA Ops:
  7.3 1.0 copy-done.5
  9.0 0.8 maximum_bitcast_fusion
  10.4 128.9 %all-gather.5.cloned.1.call-done = bf16[32,100,2048]{2,1,0:T(8,128)(2,1)} async-done(((bf16[1,100,2048]{2,1,0:T(8,128)(2,1)}), bf16[32,100,2048]{2,1,0:T(8,128)(2,1)}) %all-gather.5.cloned.1.call-update) | async-done | bytes 13107216 | tf_op jit(solution)/shard_map/all_gather | solution.py:63
  139.3 1.4 slice.56
  141.4 0.7 reshape.328
  142.1 5.3 %all-to-all-start = ((bf16[32,2,128]{2,1,0:T(2,128)(2,1)}), bf16[32,2,128]{2,1,0:T(2,128)(2,1)S(1)}, u32[]{:S(2)}, u32[]{:S(2)}) async-start(bf16[32,2,128]{2,1,0:T(2,128)(2,1)} %reshape.328), calls=%async_computation | async-start | bytes 32768 | tf_op jit(solution)/shard_map/all_to_all | solution.py:74
  147.4 16.3 %reshape.323 = bf16[3200,2048]{1,0:T(8,128)(2,1)} reshape(bf16[32,100,2048]{2,1,0:T(8,128)(2,1)} %all-gather.5.cloned.1.call-done) | data formatting | bytes 26214400
  163.8 8.7 %convolution_convert_fusion = bf16[3200,32]{0,1:T(8,128)(2,1)S(1)} fusion(bf16[3200,2048]{1,0:T(8,128)(2,1)} %reshape.323, bf16[2048,16]{0,1:T(8,128)(2,1)S(1)} %copy-done.12, bf16[2048,16]{0,1:T(8,128)(2,1)S(1)} %copy-done.13), kind=kOutput, calls=%fused_computation.5 | convolution fusion | flops 419794944 | bytes 13443072 | tf_op jit(solution)/shard_map/dot_general | solution.py:72
  172.5 1.0 all_to_all.38
  173.5 0.8 copy.52
  174.3 9.2 %all-to-all-start.1 = ((bf16[32,100,32]{1,2,0:T(8,128)(2,1)}), bf16[32,100,32]{1,2,0:T(8,128)(2,1)S(1)}, u32[]{:S(2)}, u32[]{:S(2)}) async-start(bf16[32,100,32]{1,2,0:T(8,128)(2,1)} %copy.52), calls=%async_computation.1 | async-start | bytes 524288 | tf_op jit(solution)/shard_map/all_to_all | solution.py:75
  184.4 9.6 %all-to-all-done.1 = bf16[32,100,32]{1,2,0:T(8,128)(2,1)S(1)} async-done(((bf16[32,100,32]{1,2,0:T(8,128)(2,1)}), bf16[32,100,32]{1,2,0:T(8,128)(2,1)S(1)}, u32[]{:S(2)}, u32[]{:S(2)}) %all-to-all-start.1) | async-done | bytes 204832 | tf_op jit(solution)/shard_map/all_to_all | solution.py:75
  194.1 0.8 slice.61
  195.3 5.9 %scatter_fusion = bf16[4,288,512]{2,1,0:T(8,128)(2,1)S(1)} fusion(bf16[4,288,512]{2,1,0:T(8,128)(2,1)S(1)} %bitcast.77, s32[96]{0:T(128)S(1)} %reshape.296, bf16[96,512]{1,0:T(8,128)(2,1)S(1)} %copy.53), kind=kCustom, calls=%fused_computation | custom fusion | bytes 295680 | tf_op jit(solution)/shard_map/vmap()/scatter | solution.py:26
  201.3 0.8 scatter_fusion.1
  202.0 1.6 copy.55
  203.6 1.9 fusion.2
  205.5 0.8 fusion.33
  206.5 1.0 copy.60
  207.5 5.9 %scatter_fusion.2 = bf16[4,288,512]{2,1,0:T(8,128)(2,1)S(1)} fusion(bf16[4,288,512]{2,1,0:T(8,128)(2,1)S(1)} %bitcast.75, s32[96]{0:T(128)S(1)} %reshape.296, bf16[96,512]{1,0:T(8,128)(2,1)S(1)} %copy.56), kind=kCustom, calls=%fused_computation.2 | custom fusion | bytes 295680 | tf_op jit(solution)/shard_map/vmap()/scatter | solution.py:26
  213.4 0.8 scatter_fusion.3
  214.2 1.6 copy.58
  215.8 2.2 convolution_convert_fusion.3
  218.1 12.8 %all_to_all.48 = bf16[32,2,128]{2,1,0:T(2,128)(2,1)S(1)} all-to-all(bf16[32,2,128]{2,1,0:T(2,128)(2,1)S(1)} %reshape.330), channel_id=1, replica_groups=mesh['guide'=2,'batch'=4,'tensor'=32] {'tensor'}, dimensions={0} | all-to-all | bytes 32768 | tf_op jit(solution)/shard_map/all_to_all | solution.py:119
  231.0 1.1 convolution_convert_fusion.1
  233.4 139.6 %all-reduce.3.cloned.1.call-done = bf16[128,2048]{1,0:T(8,128)(2,1)} async-done(((bf16[128,2048]{1,0:T(8,128)(2,1)}), bf16[128,2048]{1,0:T(8,128)(2,1)}) %all-reduce.3.cloned.1.call-update) | async-done | bytes 524304
  373.0 0.9 fusion.13
  374.0 0.7 fusion.20
  376.5 118.6 %all-gather.7.cloned.1.call-done = bf16[256,4,2048]{2,1,0:T(4,128)(2,1)} async-done(((bf16[1,4,2048]{2,1,0:T(4,128)(2,1)}), bf16[256,4,2048]{2,1,0:T(4,128)(2,1)}) %all-gather.7.cloned.1.call-update) | async-done | bytes 4194320 | tf_op jit(solution)/shard_map/all_gather | solution.py:130
  495.1 6.9 %reshape.325 = bf16[1024,2048]{1,0:T(8,128)(2,1)} reshape(bf16[256,4,2048]{2,1,0:T(4,128)(2,1)} %all-gather.7.cloned.1.call-done) | data formatting | bytes 8388608
  502.1 3.4 convolution_convert_fusion.2
  505.5 0.9 convert_add_fusion
  (99 shorter events, 4.9 us)
Async XLA Ops:
  7.2 494.9 %copy-start = (bf16[2048,256]{1,0:T(8,128)(2,1)S(1)}, bf16[2048,256]{1,0:T(8,128)(2,1)}, u32[]{:S(2)}) copy-start(bf16[2048,256]{1,0:T(8,128)(2,1)} %param.33) | copy-start | bytes 3145732
  7.2 132.1 %all-gather.5.cloned.1.call-start = ((), (), s32[]{:S(2)}) async-start(), calls=%async_computation.3 | async-start | bytes 14057472 | tf_op jit(solution)/shard_map/all_gather | solution.py:63
  7.2 1.1 copy-start.5
  7.2 1.3 copy-start.10
  7.3 1.5 copy-start.15
  8.3 1.5 copy-start.20
  8.3 1.6 copy-start.18
  8.3 2.1 copy-start.21
  9.0 131.9 %copy-start.7 = (bf16[2048,64]{0,1:T(8,128)(2,1)S(1)}, bf16[2048,64]{0,1:T(8,128)(2,1)}, u32[]{:S(2)}) copy-start(bf16[2048,64]{0,1:T(8,128)(2,1)} %param.29) | copy-start | bytes 786436
  9.8 131.4 %copy-start.19 = (f32[64]{0:T(128)S(1)}, f32[64]{0:T(128)}, u32[]{:S(2)}) copy-start(f32[64]{0:T(128)} %param.26) | copy-start | bytes 772
  142.1 32.2 %all-to-all-start = ((bf16[32,2,128]{2,1,0:T(2,128)(2,1)}), bf16[32,2,128]{2,1,0:T(2,128)(2,1)S(1)}, u32[]{:S(2)}, u32[]{:S(2)}) async-start(bf16[32,2,128]{2,1,0:T(2,128)(2,1)} %reshape.328), calls=%async_computation | async-start | bytes 32768 | tf_op jit(solution)/shard_map/all_to_all | solution.py:74
  147.4 16.3 %copy-start.12 = (bf16[2048,16]{0,1:T(8,128)(2,1)S(1)}, bf16[2048,16]{0,1:T(8,128)(2,1)}, u32[]{:S(2)}) copy-start(bf16[2048,16]{0,1:T(8,128)(2,1)} %param.31) | copy-start | bytes 196612
  147.4 16.3 %copy-start.13 = (bf16[2048,16]{0,1:T(8,128)(2,1)S(1)}, bf16[2048,16]{0,1:T(8,128)(2,1)}, u32[]{:S(2)}) copy-start(bf16[2048,16]{0,1:T(8,128)(2,1)} %param.30) | copy-start | bytes 196612
  163.8 19.8 %copy-start.22 = (s32[4]{0:T(128)S(1)}, s32[4]{0:T(128)}, u32[]{:S(2)}) copy-start(s32[4]{0:T(128)} %param.23) | copy-start | bytes 52
  173.5 21.8 %copy-start.4 = (bf16[1,4,288,512]{3,2,1,0:T(8,128)(2,1)S(1)}, bf16[1,4,288,512]{3,2,1,0:T(8,128)(2,1)}, u32[]{:S(2)}) copy-start(bf16[1,4,288,512]{3,2,1,0:T(8,128)(2,1)} %param.19) | copy-start | bytes 3538948
  174.3 19.6 %all-to-all-start.1 = ((bf16[32,100,32]{1,2,0:T(8,128)(2,1)}), bf16[32,100,32]{1,2,0:T(8,128)(2,1)S(1)}, u32[]{:S(2)}, u32[]{:S(2)}) async-start(bf16[32,100,32]{1,2,0:T(8,128)(2,1)} %copy.52), calls=%async_computation.1 | async-start | bytes 524288 | tf_op jit(solution)/shard_map/all_to_all | solution.py:75
  183.5 189.5 %all-reduce.3.cloned.1.call-start = ((), (), s32[]{:S(2)}) async-start(), calls=%async_computation.5 | async-start | bytes 1048576
  202.0 3.5 copy-start.3
  203.6 3.9 copy-start.2
  205.5 0.8 copy-start.8
  213.4 2.4 copy-start.9
  213.4 2.4 copy-start.24
  214.2 3.8 copy-start.1
  215.8 15.2 %copy-start.6 = (bf16[64,2048]{1,0:T(8,128)(2,1)S(1)}, bf16[64,2048]{1,0:T(8,128)(2,1)}, u32[]{:S(2)}) copy-start(bf16[64,2048]{1,0:T(8,128)(2,1)} %param.32) | copy-start | bytes 786436
  215.8 16.4 %copy-start.23 = (u32[256]{0:T(256)S(1)}, u32[256]{0:T(256)}, u32[]{:S(2)}) copy-start(u32[256]{0:T(256)} %constant.108) | copy-start | bytes 3076
  215.8 157.2 %copy-start.11 = (bf16[1,4,2048]{2,1,0:T(4,128)(2,1)S(1)}, bf16[1,4,2048]{2,1,0:T(4,128)(2,1)}, u32[]{:S(2)}) copy-start(bf16[1,4,2048]{2,1,0:T(4,128)(2,1)} %param.17) | copy-start | bytes 49156
  215.8 158.1 %copy-start.16 = (f32[2048]{0:T(1024)S(1)}, f32[2048]{0:T(1024)}, u32[]{:S(2)}) copy-start(f32[2048]{0:T(1024)} %param.28) | copy-start | bytes 24580
  215.8 158.8 %copy-start.17 = (s32[2]{0:T(128)S(1)}, s32[2]{0:T(128)}, u32[]{:S(2)}) copy-start(s32[2]{0:T(128)} %param.24) | copy-start | bytes 28
  232.1 263.0 %all-gather.7.cloned.1.call-start = ((), (), s32[]{:S(2)}) async-start(), calls=%async_computation.4 | async-start | bytes 4210688 | tf_op jit(solution)/shard_map/all_gather | solution.py:130
  373.9 128.1 %copy-start.14 = (bf16[4,2048]{1,0:T(4,128)(2,1)}, bf16[4,2048]{1,0:T(4,128)(2,1)S(1)}, u32[]{:S(2)}) copy-start(bf16[4,2048]{1,0:T(4,128)(2,1)S(1)} %get-tuple-element.9) | copy-start | bytes 49156
Sparse Core Ops, SparseCore 0:
  11.2 128.0 all-gather.4
  232.2 140.7 all-reduce.2
  377.9 117.1 all-gather.6
where the time goes:
time: 514 us; the launch traced here: 513 us
  waiting for transfers between devices  397 us (77%)
  local copies, waits for them, and re-layouts  50 us (10%)
  matrix products  17.6 us (3%)
  between operations  16.1 us (3%)
  starting transfers between devices  14.7 us (3%)
  blocking collectives  12.8 us (2%)
    unnamed x4, waiting for transfers between devices  140 us
    all_gather x1, waiting for transfers between devices, local(): gathered = lax.all_gather(kv_rows, 'tensor', axis=0, tiled=True)  129 us
    all_gather x1, waiting for transfers between devices, local(): lax.all_gather(normed_final, ('guide', 'batch', 'tensor'), axis=0, tiled=...  119 us
    unnamed x57, local copies, waits for them, and re-layouts  26 us
    scatter x7, local copies, waits for them, and re-layouts, write_rows(): return cache_one.at[pos_one].set(rows_one).at[len_one].set(row_new)  16.6 us
    all_to_all x1, blocking collectives, local(): lax.all_to_all(attended, 'tensor', split_axis=1, concat_axis=0, tiled=True)  12.8 us
  transfers between devices with their start and end apart: 5, of which 4 were waited for; matrix products, arithmetic and copies ran while one was open for 6% of the time, Pallas kernels for 0%

commit v1 on v0

v1 whole, which is shorter than its diff:
```python
import jax
import jax.numpy as jnp
from jax import lax
from jax.experimental import pallas as pl
from jax.experimental.pallas import tpu as pltpu
from jax.sharding import Mesh, PartitionSpec as P

BF = jnp.bfloat16
F32 = jnp.float32
NT = (((1,), (1,)), ((), ()))


def rms_rows(values, gain_row):
    widened = values.astype(F32)
    return (
        widened * lax.rsqrt(jnp.mean(widened * widened, axis=-1, keepdims=True) + 1e-05) * gain_row
    )


def spread(rows, axes, count):
    sent = jnp.broadcast_to(rows[None], (count,) + rows.shape)
    return lax.all_to_all(sent, axes, split_axis=0, concat_axis=0, tiled=True)


def swap_guide(values):
    return lax.ppermute(values, "guide", [(0, 1), (1, 0)])


def attend_body(
    scal_ref, kv_ref, q_ref, kgain_ref, kc_ref, vc_ref, ko_ref, vo_ref, att_ref, k_all, v_all
):
    r = pl.program_id(0)
    nrow = k_all.shape[0]
    ctx, width = kc_ref.shape[1], kc_ref.shape[2]
    old = 96

    @pl.when(r == 0)
    def _():
        m = lax.broadcasted_iota(jnp.int32, (width, width), 0)
        c = lax.broadcasted_iota(jnp.int32, (width, width), 1)
        src = ((c // 4) % 4) * 128 + (c // 16) * 4 + c % 4
        perm = (m == src).astype(F32).astype(BF)
        k_in = jnp.concatenate([kv_ref[i] for i in range(4)], axis=1)
        v_in = jnp.concatenate([kv_ref[i] for i in range(4, 8)], axis=1)
        k_raw = jnp.dot(k_in, perm, preferred_element_type=F32)
        v_all[...] = jnp.dot(v_in, perm, preferred_element_type=F32).astype(BF)
        same = (m // 64 == c // 64).astype(F32)
        mean = jnp.dot(
            k_raw * k_raw, same, preferred_element_type=F32, precision=lax.Precision.HIGHEST
        ) * (1.0 / 64)
        k_all[...] = (k_raw * lax.rsqrt(mean + 1e-05) * kgain_ref[...]).astype(BF)

    length = scal_ref[0, r]
    b0 = scal_ref[1, r] * 12
    b1 = scal_ref[2, r] * 12
    flag = scal_ref[3, r]

    i = lax.broadcasted_iota(jnp.int32, (1, nrow), 1)
    w = i - r * 24
    pos = jnp.where(w < 12, b0 + w, b1 + w - 12)
    pos = jnp.where((w >= 0) & (w < 24) & (i < old), pos, -1)
    pos = jnp.where(i == old + r, length, pos)
    j = lax.broadcasted_iota(jnp.int32, (ctx, nrow), 0)
    sel = (j == pos).astype(F32).astype(BF)
    jr = lax.broadcasted_iota(jnp.int32, (ctx, 1), 0)
    hit = (
        ((jr >= b0) & (jr < b0 + 12)) | ((jr >= b1) & (jr < b1 + 12)) | (jr == length)
    )
    new_k = jnp.dot(sel, k_all[...], preferred_element_type=F32)
    new_k = jnp.where(hit, new_k, kc_ref[0].astype(F32)).astype(BF)
    ko_ref[0] = new_k
    new_v = jnp.dot(sel, v_all[...], preferred_element_type=F32)
    new_v = jnp.where(hit, new_v, vc_ref[0].astype(F32)).astype(BF)
    vo_ref[0] = new_v

    heads = q_ref.shape[0]
    lq = lax.broadcasted_iota(jnp.int32, (q_ref.shape[1], width), 0)
    cq = lax.broadcasted_iota(jnp.int32, (q_ref.shape[1], width), 1)
    tile = (lq == r * 64 + cq % 64).astype(F32).astype(BF)
    h = lax.broadcasted_iota(jnp.int32, (heads, width), 0)
    ch = lax.broadcasted_iota(jnp.int32, (heads, width), 1)
    own = h // 4 == ch // 64
    q_wide = jnp.where(own, jnp.dot(q_ref[...], tile, preferred_element_type=F32), 0.0).astype(BF)
    scores = lax.dot_general(q_wide, new_k, NT, preferred_element_type=F32) * 0.125
    col = lax.broadcasted_iota(jnp.int32, (heads, ctx), 1)
    visible = ((col < length) & (flag == 0)) | (col == length)
    scores = jnp.where(visible, scores, -1e30)
    top = jnp.max(scores, axis=-1, keepdims=True)
    powers = jnp.exp(scores - top)
    probs = (powers / jnp.sum(powers, axis=-1, keepdims=True)).astype(BF)
    wide = jnp.where(own, jnp.dot(probs, new_v, preferred_element_type=F32), 0.0).astype(BF)
    gh = lax.broadcasted_iota(jnp.int32, (4, heads), 0)
    hh = lax.broadcasted_iota(jnp.int32, (4, heads), 1)
    pick = (hh % 4 == gh).astype(F32).astype(BF)
    att_ref[0] = jnp.dot(pick, wide, preferred_element_type=F32).astype(BF)


def attend(scal, kv_back, q_all, kgain, key_cache, value_cache):
    n, ctx, width = key_cache.shape
    nrow = kv_back.shape[1]
    whole = lambda a: pl.BlockSpec(a.shape, lambda r, s: (0,) * a.ndim)
    one = pl.BlockSpec((1, ctx, width), lambda r, s: (r, 0, 0))
    return pl.pallas_call(
        attend_body,
        grid_spec=pltpu.PrefetchScalarGridSpec(
            num_scalar_prefetch=1,
            grid=(n,),
            in_specs=[whole(kv_back), whole(q_all), whole(kgain), one, one],
            out_specs=[one, one, pl.BlockSpec((1, 4, width), lambda r, s: (r, 0, 0))],
            scratch_shapes=[pltpu.VMEM((nrow, width), BF), pltpu.VMEM((nrow, width), BF)],
        ),
        out_shape=[
            jax.ShapeDtypeStruct(key_cache.shape, BF),
            jax.ShapeDtypeStruct(value_cache.shape, BF),
            jax.ShapeDtypeStruct((n, 4, width), BF),
        ],
        compiler_params=pltpu.CompilerParams(vmem_limit_bytes=40 << 20),
        name="attend",
    )(scal, kv_back, q_all, kgain, key_cache, value_cache)


def local(
    hidden_new,
    stored_rows,
    key_cache,
    value_cache,
    lengths,
    recompute_blocks,
    prefill_flags,
    guidance,
    attn_gain,
    query_gain,
    key_gain,
    final_gain,
    w_query,
    w_key,
    w_value,
    w_out,
    w_vocab,
):
    width = hidden_new.shape[2]
    side = lax.axis_index("guide")
    eighth = side * 4 + lax.axis_index("batch")
    x_rows = hidden_new[0]
    normed_new = rms_rows(x_rows, attn_gain).astype(BF)

    kv_cols = jnp.concatenate([w_key.T, w_value.T], axis=0)
    kv_eighth = lax.dynamic_slice_in_dim(kv_cols, eighth * 4, 4, 0)
    got = spread(jnp.concatenate([kv_eighth, normed_new], axis=0), ("z", "y"), 32)
    kv_w = got[:, :4].reshape(128, width)

    normed_old = rms_rows(stored_rows[0], attn_gain).astype(BF).reshape(96, width)
    kv_rows = jnp.concatenate([normed_old, normed_new, jnp.zeros((4, width), BF)], axis=0)
    rows_mine = spread(kv_rows, "batch", 4)
    rows_other = swap_guide(rows_mine)
    dot_kv = lambda a: lax.dot_general(
        a.reshape(416, width), kv_w, NT, preferred_element_type=F32
    ).astype(BF).reshape(1, 4, 104, 128)
    kv_mine, kv_other = dot_kv(rows_mine), dot_kv(rows_other)
    kv_sent = jnp.where(
        side == 0,
        jnp.concatenate([kv_mine, kv_other], axis=0),
        jnp.concatenate([kv_other, kv_mine], axis=0),
    ).reshape(8, 104, 128)
    kv_back = lax.all_to_all(
        kv_sent, ("guide", "batch"), split_axis=0, concat_axis=0, tiled=True
    )

    q_raw = jnp.dot(got.reshape(256, width), w_query, preferred_element_type=F32)
    q_raw = q_raw.reshape(32, 8, 64)[:, 4:]
    q_part = rms_rows(q_raw, query_gain).astype(BF).reshape(32, 2, 128)
    q_all = lax.all_to_all(q_part, ("z", "y"), split_axis=0, concat_axis=0, tiled=True)
    q_all = q_all.reshape(32, 256)

    scal = jnp.concatenate(
        [lengths, recompute_blocks[0].T, prefill_flags[None]], axis=0
    )
    kgain = jnp.tile(key_gain, 8)[None]
    new_keys, new_values, att = attend(scal, kv_back, q_all, kgain, key_cache[0], value_cache[0])

    wo_eighth = lax.dynamic_slice_in_dim(w_out, eighth * 256, 256, 1)
    wo = spread(wo_eighth, ("y", "z"), 32).reshape(width, 256)
    att_all = spread(att.reshape(16, 512), ("guide", "batch"), 8).reshape(32, width)
    proj = jnp.dot(att_all, wo, preferred_element_type=F32).reshape(8, 4, 256)
    proj = lax.all_to_all(proj, ("guide", "batch"), split_axis=0, concat_axis=0, tiled=True)
    projected = proj.transpose(1, 0, 2).reshape(4, width)
    residual = (x_rows.astype(F32) + projected).astype(BF)

    weight = guidance[0].astype(F32) / guidance[1].astype(F32)
    final = rms_rows(residual, final_gain) * jnp.where(side == 0, weight, 1.0 - weight)
    half = width // 2
    keep = lax.dynamic_slice_in_dim(final, side * half, half, 1)
    give = lax.dynamic_slice_in_dim(final, (1 - side) * half, half, 1)
    both = (keep + swap_guide(give)).astype(BF)
    both = spread(both, "z", 8).reshape(32, half)
    rows_half = spread(both, ("batch", "y"), 16).reshape(512, half)
    rows_rest = swap_guide(rows_half)
    w_half = lax.dynamic_slice_in_dim(w_vocab, side * half, half, 0)
    w_rest = lax.dynamic_slice_in_dim(w_vocab, (1 - side) * half, half, 0)
    guided = jnp.dot(rows_half, w_half, preferred_element_type=F32) + jnp.dot(
        rows_rest, w_rest, preferred_element_type=F32
    )
    guided = guided.reshape(4, 4, 8, 4, 256).transpose(0, 2, 1, 3, 4).reshape(512, 256)
    return (residual[None], new_keys[None], new_values[None], guided)


def solution(mesh):
    mesh = Mesh(mesh.devices.reshape(2, 4, 8, 4), ("guide", "batch", "z", "y"))
    tensor = ("z", "y")
    rows = ("batch", "z", "y")
    in_specs = (
        P("guide", rows, None),
        P("guide", rows, None, None),
        P("guide", rows, None, None),
        P("guide", rows, None, None),
        P("guide", rows),
        P("guide", rows, None),
        P(rows),
        P(),
        P(),
        P(),
        P(),
        P(),
        P(None, tensor),
        P(None, tensor),
        P(None, tensor),
        P(tensor, None),
        P(None, ("guide",) + rows),
    )
    out_specs = (
        P("guide", rows, None),
        P("guide", rows, None, None),
        P("guide", rows, None, None),
        P(None, ("guide",) + rows),
    )
    return jax.shard_map(local, mesh=mesh, in_specs=in_specs, out_specs=out_specs, check_vma=False)
```

time: 514 us -> 202 us (0.39)
  waiting for transfers between devices: 397 us -> 87.3 us
  local copies, waits for them, and re-layouts: 50 us -> 8.52 us
  starting transfers between devices: 14.7 us -> 54.5 us
  blocking collectives: 12.8 us -> 28.7 us
  between operations: 16.1 us -> 2.27 us
  matrix products: 17.6 us -> 6.73 us
  Pallas kernels: 0 us -> 6.69 us
    all_gather x2 -> x0, waiting for transfers between devices: 247 us -> none  [the longest x1 129 us: local(): gathered = lax.all_gather(kv_rows, 'tensor', axis=0, tiled=True)]
    unnamed x4 -> x0, waiting for transfers between devices: 140 us -> none
    all_to_all x2 -> x7, waiting for transfers between devices: 9.56 us -> 85.2 us  [the longest x4 72.9 us: spread(): return lax.all_to_all(sent, axes, split_axis=0, concat_axis=0, tiled=True)]
    all_to_all x2 -> x7, starting transfers between devices: 14.5 us -> 49 us  [the longest x4 27.4 us: spread(): return lax.all_to_all(sent, axes, split_axis=0, concat_axis=0, tiled=True)]
    unnamed x57 -> x31, local copies, waits for them, and re-layouts: 26 us -> 0.16 us
    scatter x7 -> x0, local copies, waits for them, and re-layouts: 16.6 us -> none  [write_rows(): return cache_one.at[pos_one].set(rows_one).at[len_one].set(row_new)]
    all_to_all x1 -> x2, blocking collectives: 12.8 us -> 28.7 us  [spread(): return lax.all_to_all(sent, axes, split_axis=0, concat_axis=0, tiled=True)]
    dot_general x6, matrix products: 17.6 us -> 6.73 us  [the longest x2 4.38 us: local(): lax.dot_general(a.reshape(416, width), kv_w, NT, preferred_element_type=F32)]
  transfers between devices with their start and end apart: 5 -> 10, of which waited for: 4 -> 9; matrix products, arithmetic and copies ran while one was open for 6% -> 5% of each run, Pallas kernels for 0% -> 0%
where the time goes in v1:
time: 202 us; the launch traced here: 201 us
  waiting for transfers between devices  87.3 us (43%)
  starting transfers between devices  54.5 us (27%)
  blocking collectives  28.7 us (14%)
  local copies, waits for them, and re-layouts  8.52 us (4%)
  matrix products  6.73 us (3%)
  Pallas kernels  6.69 us (3%)
  other arithmetic  5.95 us (3%)
  between operations  2.27 us (1%)
    all_to_all x4, waiting for transfers between devices, spread(): return lax.all_to_all(sent, axes, split_axis=0, concat_axis=0, tiled=True)  72.9 us
    all_to_all x2, blocking collectives, spread(): return lax.all_to_all(sent, axes, split_axis=0, concat_axis=0, tiled=True)  28.7 us
    all_to_all x4, starting transfers between devices, spread(): return lax.all_to_all(sent, axes, split_axis=0, concat_axis=0, tiled=True)  27.4 us
    all_to_all x1, starting transfers between devices, local(): lax.all_to_all(proj, ('guide', 'batch'), split_axis=0, concat_axis=0, til...  7.61 us
    all_to_all x1, starting transfers between devices, local(): lax.all_to_all(kv_sent, ('guide', 'batch'), split_axis=0, concat_axis=0,...  7.37 us
    pallas_call x1, Pallas kernels, attend(): pl.pallas_call(attend_body, grid_spec=pltpu.PrefetchScalarGridSpec(num_sc...  6.69 us
    all_to_all x1, starting transfers between devices, local(): lax.all_to_all(q_part, ('z', 'y'), split_axis=0, concat_axis=0, tiled=True)  6.67 us
    all_to_all x1, waiting for transfers between devices, local(): lax.all_to_all(kv_sent, ('guide', 'batch'), split_axis=0, concat_axis=0,...  6.02 us
  transfers between devices with their start and end apart: 10, of which 9 were waited for; matrix products, arithmetic and copies ran while one was open for 5% of the time, Pallas kernels for 0%

profile of v1, /device:TPU:1, one launch (start us, length us, event | category | flops | bytes accessed | tf_op | source)
XLA Modules:
  0.0 200.6 jit_solution(5310058282774860151)
XLA Ops:
  0.6 0.9 fusion.9
  1.6 1.1 multiply_reduce_fusion
  2.8 0.8 fusion.11
  3.7 1.2 fusion.1
  5.1 1.4 broadcast_in_dim.26
  6.5 5.0 %all-to-all-start = ((bf16[4,104,2048]{2,1,0:T(8,128)(2,1)}), bf16[4,104,2048]{2,1,0:T(8,128)(2,1)}, u32[]{:S(2)}, u32[]{:S(2)}) async-start(bf16[4,104,2048]{2,1,0:T(8,128)(2,1)} %broadcast_in_dim.26), calls=%async_computation | async-start | bytes 3407872 | tf_op jit(solution)/shard_map/all_to_all | solution.py:22
  11.5 19.7 %all-to-all-done = bf16[4,104,2048]{2,1,0:T(8,128)(2,1)} async-done(((bf16[4,104,2048]{2,1,0:T(8,128)(2,1)}), bf16[4,104,2048]{2,1,0:T(8,128)(2,1)}, u32[]{:S(2)}, u32[]{:S(2)}) %all-to-all-start) | async-done | bytes 1703968 | tf_op jit(solution)/shard_map/all_to_all | solution.py:22
  31.2 1.1 broadcast_in_dim.27
  32.3 13.5 %all-to-all-start.1 = ((bf16[32,8,2048]{2,1,0:T(8,128)(2,1)}), bf16[32,8,2048]{2,1,0:T(8,128)(2,1)S(1)}, u32[]{:S(2)}, u32[]{:S(2)}) async-start(bf16[32,8,2048]{2,1,0:T(8,128)(2,1)} %broadcast_in_dim.27), calls=%async_computation.1 | async-start | bytes 2097152 | tf_op jit(solution)/shard_map/all_to_all | solution.py:22
  45.8 1.9 collective-permute-start
  47.7 23.7 %all-to-all-done.1 = bf16[32,8,2048]{2,1,0:T(8,128)(2,1)S(1)} async-done(((bf16[32,8,2048]{2,1,0:T(8,128)(2,1)}), bf16[32,8,2048]{2,1,0:T(8,128)(2,1)S(1)}, u32[]{:S(2)}, u32[]{:S(2)}) %all-to-all-start.1) | async-done | bytes 1048608 | tf_op jit(solution)/shard_map/all_to_all | solution.py:22
  73.3 6.7 %all-to-all-start.3 = ((bf16[32,2,128]{2,1,0:T(2,128)(2,1)}), bf16[32,2,128]{2,1,0:T(2,128)(2,1)S(1)}, u32[]{:S(2)}, u32[]{:S(2)}) async-start(bf16[32,2,128]{2,1,0:T(2,128)(2,1)} %reshape.130), calls=%async_computation.3 | async-start | bytes 32768 | tf_op jit(solution)/shard_map/all_to_all | solution.py:172
  80.0 2.1 %convolution_convert_fusion.1 = bf16[416,128]{1,0:T(8,128)(2,1)S(1)} fusion(bf16[416,2048]{1,0:T(8,128)(2,1)} %bitcast.5, bf16[128,2048]{1,0:T(8,128)(2,1)S(1)} %reshape.126), kind=kOutput, calls=%fused_computation.2 | convolution fusion | flops 218157056 | bytes 2334720 | tf_op jit(solution)/shard_map/dot_general | solution.py:156
  82.2 2.3 %convolution_convert_fusion = bf16[416,128]{1,0:T(8,128)(2,1)S(1)} fusion(bf16[416,2048]{1,0:T(8,128)(2,1)} %bitcast.9, bf16[128,2048]{1,0:T(8,128)(2,1)} %copy-done.3), kind=kOutput, calls=%fused_computation.1 | convolution fusion | flops 218157056 | bytes 2334720 | tf_op jit(solution)/shard_map/dot_general | solution.py:156
  85.2 3.3 %all-to-all-done.3 = bf16[32,2,128]{2,1,0:T(2,128)(2,1)S(1)} async-done(((bf16[32,2,128]{2,1,0:T(2,128)(2,1)}), bf16[32,2,128]{2,1,0:T(2,128)(2,1)S(1)}, u32[]{:S(2)}, u32[]{:S(2)}) %all-to-all-start.3) | async-done | bytes 16416 | tf_op jit(solution)/shard_map/all_to_all | solution.py:172
  88.5 7.4 %all-to-all-start.2 = ((bf16[8,104,128]{2,1,0:T(8,128)(2,1)}), bf16[8,104,128]{2,1,0:T(8,128)(2,1)}, u32[]{:S(2)}, u32[]{:S(2)}) async-start(bf16[8,104,128]{2,1,0:T(8,128)(2,1)} %bitcast.77), calls=%async_computation.2 | async-start | bytes 425984 | tf_op jit(solution)/shard_map/all_to_all | solution.py:165
  96.0 6.0 %all-to-all-done.2.kv_ref = bf16[8,104,128]{2,1,0:T(8,128)(2,1)} async-done(((bf16[8,104,128]{2,1,0:T(8,128)(2,1)}), bf16[8,104,128]{2,1,0:T(8,128)(2,1)}, u32[]{:S(2)}, u32[]{:S(2)}) %all-to-all-start.2) | async-done | bytes 213024 | tf_op jit(solution)/shard_map/all_to_all | solution.py:165
  102.0 6.7 %attend.1 = (bf16[4,288,512]{2,1,0:T(8,128)(2,1)}, bf16[4,288,512]{2,1,0:T(8,128)(2,1)}, bf16[4,4,512]{2,1,0:T(4,128)(2,1)S(1)}) custom-call(s32[4,4]{1,0:T(4,128)S(1)} %pad_add_fusion.scal_ref, bf16[8,104,128]{2,1,0:T(8,128)(2,1)} %all-to-all-done.2.kv_ref, bf16[32,256]{1,0:T(8,128)(2,1)S(1)} %bitcast.72, f32[1,512]{1,0:T(1,128)S(1)} %broadcast_in_dim_tile.3.kgain_ref, ...), custom_call_target="tpu_custom_call" | custom-call | tf_op jit(solution)/shard_map/attend/pallas_call | solution.py:103
  109.4 3.7 %all-to-all-start.4 = ((bf16[8,16,512]{2,1,0:T(8,128)(2,1)}), bf16[8,16,512]{2,1,0:T(8,128)(2,1)S(1)}, u32[]{:S(2)}, u32[]{:S(2)}) async-start(bf16[8,16,512]{2,1,0:T(8,128)(2,1)} %broadcast_in_dim.29), calls=%async_computation.4 | async-start | bytes 262144 | tf_op jit(solution)/shard_map/all_to_all | solution.py:22
  113.9 4.4 %all-to-all-done.4 = bf16[8,16,512]{2,1,0:T(8,128)(2,1)S(1)} async-done(((bf16[8,16,512]{2,1,0:T(8,128)(2,1)}), bf16[8,16,512]{2,1,0:T(8,128)(2,1)S(1)}, u32[]{:S(2)}, u32[]{:S(2)}) %all-to-all-start.4) | async-done | bytes 131104 | tf_op jit(solution)/shard_map/all_to_all | solution.py:22
  118.3 1.1 broadcast_in_dim.30
  119.4 5.2 %all-to-all-start.5 = ((bf16[32,64,256]{2,1,0:T(8,128)(2,1)}), bf16[32,64,256]{2,1,0:T(8,128)(2,1)S(1)}, u32[]{:S(2)}, u32[]{:S(2)}) async-start(bf16[32,64,256]{2,1,0:T(8,128)(2,1)} %broadcast_in_dim.30), calls=%async_computation.5 | async-start | bytes 2097152 | tf_op jit(solution)/shard_map/all_to_all | solution.py:22
  124.7 25.1 %all-to-all-done.5 = bf16[32,64,256]{2,1,0:T(8,128)(2,1)S(1)} async-done(((bf16[32,64,256]{2,1,0:T(8,128)(2,1)}), bf16[32,64,256]{2,1,0:T(8,128)(2,1)S(1)}, u32[]{:S(2)}, u32[]{:S(2)}) %all-to-all-start.5) | async-done | bytes 1048608 | tf_op jit(solution)/shard_map/all_to_all | solution.py:22
  149.8 0.9 fusion.17
  150.7 7.6 %all-to-all-start.6 = ((f32[8,4,256]{2,1,0:T(4,128)}), f32[8,4,256]{2,1,0:T(4,128)S(1)}, u32[]{:S(2)}, u32[]{:S(2)}) async-start(f32[8,4,256]{2,1,0:T(4,128)} %fusion.17), calls=%async_computation.6 | async-start | bytes 65536 | tf_op jit(solution)/shard_map/all_to_all | solution.py:185
  160.2 3.0 %all-to-all-done.6 = f32[8,4,256]{2,1,0:T(4,128)S(1)} async-done(((f32[8,4,256]{2,1,0:T(4,128)}), f32[8,4,256]{2,1,0:T(4,128)S(1)}, u32[]{:S(2)}, u32[]{:S(2)}) %all-to-all-start.6) | async-done | bytes 32800 | tf_op jit(solution)/shard_map/all_to_all | solution.py:185
  163.9 0.8 collective-permute-done.1
  164.8 10.5 %all_to_all.45 = bf16[8,4,1024]{2,1,0:T(4,128)(2,1)S(1)} all-to-all(bf16[8,4,1024]{2,1,0:T(4,128)(2,1)S(1)} %broadcast_in_dim.33), channel_id=1, replica_groups=mesh['guide'=2,'batch'=4,'z'=8,'y'=4] {'z'}, dimensions={0} | all-to-all | bytes 131072 | tf_op jit(solution)/shard_map/all_to_all | solution.py:22
  175.4 18.2 %all_to_all.46 = bf16[16,32,1024]{2,1,0:T(8,128)(2,1)S(1)} all-to-all(bf16[16,32,1024]{2,1,0:T(8,128)(2,1)S(1)} %broadcast_in_dim.70), channel_id=1, replica_groups=mesh['guide'=2,'batch'=4,'z'=8,'y'=4] {'batch','y'}, dimensions={0} | all-to-all | bytes 2097152 | tf_op jit(solution)/shard_map/all_to_all | solution.py:22
  193.6 3.1 %collective-permute-start.2 = (bf16[512,1024]{1,0:T(8,128)(2,1)S(1)}, bf16[512,1024]{1,0:T(8,128)(2,1)S(1)}, u32[]{:S(2)}, u32[]{:S(2)}) collective-permute-start(bf16[512,1024]{1,0:T(8,128)(2,1)S(1)} %bitcast.73), channel_id=1, source_target_pairs={{0,128},{128,0},{1,129},{129,1},{2,130},{130,2},{3,131},{131,3},{4... | collective-permute-start | bytes 3145736 | tf_op jit(solution)/shard_map/ppermute | solution.py:26
  197.7 1.2 collective-permute-done.2
  199.6 1.0 reshape.137
  (69 shorter events, 7.8 us)
Async XLA Ops:
  0.6 196.7 %copy-start = (bf16[2048,256]{1,0:T(8,128)(2,1)S(1)}, bf16[2048,256]{1,0:T(8,128)(2,1)}, u32[]{:S(2)}) copy-start(bf16[2048,256]{1,0:T(8,128)(2,1)} %param.33) | copy-start | bytes 3145732
  6.5 5.0 %copy-start.5 = (bf16[2048,16]{0,1:T(8,128)(2,1)S(1)}, bf16[2048,16]{0,1:T(8,128)(2,1)}, u32[]{:S(2)}) copy-start(bf16[2048,16]{0,1:T(8,128)(2,1)} %param.30) | copy-start | bytes 196612
  6.5 5.0 %copy-start.6 = (bf16[2048,16]{0,1:T(8,128)(2,1)S(1)}, bf16[2048,16]{0,1:T(8,128)(2,1)}, u32[]{:S(2)}) copy-start(bf16[2048,16]{0,1:T(8,128)(2,1)} %param.31) | copy-start | bytes 196612
  6.5 24.7 %all-to-all-start = ((bf16[4,104,2048]{2,1,0:T(8,128)(2,1)}), bf16[4,104,2048]{2,1,0:T(8,128)(2,1)}, u32[]{:S(2)}, u32[]{:S(2)}) async-start(bf16[4,104,2048]{2,1,0:T(8,128)(2,1)} %broadcast_in_dim.26), calls=%async_computation | async-start | bytes 3407872 | tf_op jit(solution)/shard_map/all_to_all | solution.py:22
  32.3 39.5 %copy-start.14 = (bf16[2048,64]{0,1:T(8,128)(2,1)S(1)}, bf16[2048,64]{0,1:T(8,128)(2,1)}, u32[]{:S(2)}) copy-start(bf16[2048,64]{0,1:T(8,128)(2,1)} %param.29) | copy-start | bytes 786436
  32.3 39.2 %all-to-all-start.1 = ((bf16[32,8,2048]{2,1,0:T(8,128)(2,1)}), bf16[32,8,2048]{2,1,0:T(8,128)(2,1)S(1)}, u32[]{:S(2)}, u32[]{:S(2)}) async-start(bf16[32,8,2048]{2,1,0:T(8,128)(2,1)} %broadcast_in_dim.27), calls=%async_computation.1 | async-start | bytes 2097152 | tf_op jit(solution)/shard_map/all_to_all | solution.py:22
  45.8 36.3 %collective-permute-start = (bf16[4,104,2048]{2,1,0:T(8,128)(2,1)}, bf16[4,104,2048]{2,1,0:T(8,128)(2,1)}, u32[]{:S(2)}, u32[]{:S(2)}) collective-permute-start(bf16[4,104,2048]{2,1,0:T(8,128)(2,1)} %all-to-all-done), channel_id=1, source_target_pairs={{0,128},{128,0},{1,129},{129,1},{2,130},{130,2},{3,131},{131,3},{4... | collective-permute-start | bytes 5111816 | tf_op jit(solution)/shard_map/ppermute | solution.py:26
  71.8 8.2 %copy-start.3 = (bf16[128,2048]{1,0:T(8,128)(2,1)}, bf16[128,2048]{1,0:T(8,128)(2,1)S(1)}, u32[]{:S(2)}) copy-start(bf16[128,2048]{1,0:T(8,128)(2,1)S(1)} %reshape.126) | copy-start | bytes 1572868
  71.8 0.7 copy-start.10
  73.3 15.2 %all-to-all-start.3 = ((bf16[32,2,128]{2,1,0:T(2,128)(2,1)}), bf16[32,2,128]{2,1,0:T(2,128)(2,1)S(1)}, u32[]{:S(2)}, u32[]{:S(2)}) async-start(bf16[32,2,128]{2,1,0:T(2,128)(2,1)} %reshape.130), calls=%async_computation.3 | async-start | bytes 32768 | tf_op jit(solution)/shard_map/all_to_all | solution.py:172
  82.1 13.8 %copy-start.11 = (f32[64]{0:T(128)S(1)}, f32[64]{0:T(128)}, u32[]{:S(2)}) copy-start(f32[64]{0:T(128)} %param.27) | copy-start | bytes 772
  82.1 13.9 %copy-start.9 = (s32[1,4,2]{1,2,0:T(2,128)S(1)}, s32[1,4,2]{1,2,0:T(2,128)}, u32[]{:S(2)}) copy-start(s32[1,4,2]{1,2,0:T(2,128)} %param.22) | copy-start | bytes 100
  82.1 13.9 %copy-start.12 = (s32[4]{0:T(128)S(1)}, s32[4]{0:T(128)}, u32[]{:S(2)}) copy-start(s32[4]{0:T(128)} %param.23) | copy-start | bytes 52
  82.1 13.9 %copy-start.13 = (s32[1,4]{1,0:T(1,128)S(1)}, s32[1,4]{1,0:T(1,128)}, u32[]{:S(2)}) copy-start(s32[1,4]{1,0:T(1,128)} %param.21) | copy-start | bytes 52
  82.1 19.9 %copy-start.1 = (bf16[1,4,288,512]{3,2,1,0:T(8,128)(2,1)S(1)}, bf16[1,4,288,512]{3,2,1,0:T(8,128)(2,1)}, u32[]{:S(2)}) copy-start(bf16[1,4,288,512]{3,2,1,0:T(8,128)(2,1)} %param.19) | copy-start | bytes 3538948
  82.1 19.9 %copy-start.2 = (bf16[1,4,288,512]{3,2,1,0:T(8,128)(2,1)S(1)}, bf16[1,4,288,512]{3,2,1,0:T(8,128)(2,1)}, u32[]{:S(2)}) copy-start(bf16[1,4,288,512]{3,2,1,0:T(8,128)(2,1)} %param.20) | copy-start | bytes 3538948
  88.5 13.5 %all-to-all-start.2 = ((bf16[8,104,128]{2,1,0:T(8,128)(2,1)}), bf16[8,104,128]{2,1,0:T(8,128)(2,1)}, u32[]{:S(2)}, u32[]{:S(2)}) async-start(bf16[8,104,128]{2,1,0:T(8,128)(2,1)} %bitcast.77), calls=%async_computation.2 | async-start | bytes 425984 | tf_op jit(solution)/shard_map/all_to_all | solution.py:165
  109.4 8.8 %all-to-all-start.4 = ((bf16[8,16,512]{2,1,0:T(8,128)(2,1)}), bf16[8,16,512]{2,1,0:T(8,128)(2,1)S(1)}, u32[]{:S(2)}, u32[]{:S(2)}) async-start(bf16[8,16,512]{2,1,0:T(8,128)(2,1)} %broadcast_in_dim.29), calls=%async_computation.4 | async-start | bytes 262144 | tf_op jit(solution)/shard_map/all_to_all | solution.py:22
  119.4 38.9 %copy-start.8 = (s32[2]{0:T(128)S(1)}, s32[2]{0:T(128)}, u32[]{:S(2)}) copy-start(s32[2]{0:T(128)} %param.24) | copy-start | bytes 28
  119.4 43.8 %copy-start.4 = (bf16[1,4,2048]{2,1,0:T(4,128)(2,1)S(1)}, bf16[1,4,2048]{2,1,0:T(4,128)(2,1)}, u32[]{:S(2)}) copy-start(bf16[1,4,2048]{2,1,0:T(4,128)(2,1)} %param.17) | copy-start | bytes 49156
  119.4 44.0 %copy-start.7 = (f32[2048]{0:T(1024)S(1)}, f32[2048]{0:T(1024)}, u32[]{:S(2)}) copy-start(f32[2048]{0:T(1024)} %param.28) | copy-start | bytes 24580
  119.4 30.4 %all-to-all-start.5 = ((bf16[32,64,256]{2,1,0:T(8,128)(2,1)}), bf16[32,64,256]{2,1,0:T(8,128)(2,1)S(1)}, u32[]{:S(2)}, u32[]{:S(2)}) async-start(bf16[32,64,256]{2,1,0:T(8,128)(2,1)} %broadcast_in_dim.30), calls=%async_computation.5 | async-start | bytes 2097152 | tf_op jit(solution)/shard_map/all_to_all | solution.py:22
  150.7 12.5 %all-to-all-start.6 = ((f32[8,4,256]{2,1,0:T(4,128)}), f32[8,4,256]{2,1,0:T(4,128)S(1)}, u32[]{:S(2)}, u32[]{:S(2)}) async-start(f32[8,4,256]{2,1,0:T(4,128)} %fusion.17), calls=%async_computation.6 | async-start | bytes 65536 | tf_op jit(solution)/shard_map/all_to_all | solution.py:185
  163.4 1.3 collective-permute-start.1
  193.6 5.4 %collective-permute-start.2 = (bf16[512,1024]{1,0:T(8,128)(2,1)S(1)}, bf16[512,1024]{1,0:T(8,128)(2,1)S(1)}, u32[]{:S(2)}, u32[]{:S(2)}) collective-permute-start(bf16[512,1024]{1,0:T(8,128)(2,1)S(1)} %bitcast.73), channel_id=1, source_target_pairs={{0,128},{128,0},{1,129},{129,1},{2,130},{130,2},{3,131},{131,3},{4... | collective-permute-start | bytes 3145736 | tf_op jit(solution)/shard_map/ppermute | solution.py:26
